TPU v7x, 32 devices: a whole 2x2x4 slice. The times are simulated.
32 devices in a mesh: dp: 8 (over z, x), tensor: 4 (over y, core).
Axes of the slice: x: 2, y: 2, z: 4, core: 2. Of those that a mesh axis runs over, the one named last changes fastest.
Arguments:
- context: bfloat16 [2, 8192, 3072], P(None, 'dp', 'tensor'), may hold values from -6 to 6
- out_grad: bfloat16 [2, 8192, 3072], P(None, ('dp', 'tensor')), may hold values from -0.1875 to 0.1875
- error_in: bfloat16 [2, 24576, 3072], P(None, 'dp', 'tensor'), may hold values from -6 to 6
- right_init: float32 [2, 64, 3072], P(None, None, 'tensor'), may hold values from -6 to 6
Outputs:
- summed_update: bfloat16 [2, 3072, 3072], P(None, 'dp', 'tensor')
- error_out: bfloat16 [2, 24576, 3072], P(None, 'dp', 'tensor')
All inputs are finite; a program needn't handle non-finite values.
Results may differ from a plain program's by a relative error of at most 0.015.
Values may be sent and summed in bfloat16 or wider, within the bound.
A program may use at most 128 MiB of HBM per device.

v0:
```python
import jax
import jax.numpy as jnp
from jax import lax
from jax.sharding import PartitionSpec as P


def solve_rows(gram_matrix, left_factor):
    ridge_term = 1e-06 * jnp.mean(jnp.diagonal(gram_matrix, axis1=1, axis2=2), axis=1)
    eye_matrix = jnp.eye(gram_matrix.shape[1], dtype=gram_matrix.dtype)
    gram_matrix = gram_matrix + ridge_term[:, None, None] * eye_matrix
    factor_low = jnp.linalg.cholesky(gram_matrix)

    def one_solve(low_part, rhs_part):
        return jax.scipy.linalg.solve_triangular(low_part, rhs_part, lower=True)

    return jax.vmap(one_solve)(factor_low, left_factor)


def gram_of(left_factor):
    return jnp.einsum("lrd,lsd->lrs", left_factor, left_factor, precision=lax.Precision.HIGHEST)


def compress(context, out_grad, error_in, right_init):
    out_width = out_grad.shape[2]
    moment = jnp.einsum(
        "ltd,lte->lde",
        lax.all_gather(out_grad, "tensor", axis=1, tiled=True),
        context,
        preferred_element_type=jnp.float32,
    )
    moment = moment + error_in.astype(jnp.float32)
    left_factor = jnp.einsum("lre,lde->lrd", right_init, moment, precision=lax.Precision.HIGHEST)
    left_part = lax.psum_scatter(left_factor, "tensor", scatter_dimension=2, tiled=True)
    left_part = lax.psum(left_part, "dp")
    gram_matrix = lax.psum(gram_of(left_part), "tensor")
    ortho_part = solve_rows(gram_matrix, left_part)
    ortho_basis = lax.all_gather(ortho_part, "tensor", axis=2, tiled=True)
    right_terms = jnp.einsum("lrd,lde->lre", ortho_basis, moment, precision=lax.Precision.HIGHEST)
    right_factor = lax.psum(right_terms.astype(jnp.bfloat16), "dp").astype(jnp.float32)
    replicas = lax.axis_size("dp")
    row_share = out_width // replicas
    own_basis = lax.dynamic_slice_in_dim(
        ortho_basis, lax.axis_index("dp") * row_share, row_share, 2
    )
    summed = jnp.einsum("lrd,lre->lde", own_basis, right_factor, precision=lax.Precision.HIGHEST)
    mean_part = jnp.einsum(
        "lrd,lre->lde", ortho_basis, right_factor / replicas, precision=lax.Precision.HIGHEST
    )
    new_error = (moment - mean_part).astype(jnp.bfloat16)
    return (summed.astype(jnp.bfloat16), new_error)


def body(context, out_grad, error_in, right_init):
    return compress(context, out_grad, error_in, right_init)


def solution(mesh):
    return jax.shard_map(
        body,
        mesh=mesh,
        in_specs=(
            P(None, "dp", "tensor"),
            P(None, ("dp", "tensor"), None),
            P(None, "dp", "tensor"),
            P(None, None, "tensor"),
        ),
        out_specs=(P(None, "dp", "tensor"), P(None, "dp", "tensor")),
        check_vma=False,
    )
```

profile of v0, /device:TPU:0, one launch (start us, length us, event | category | flops | bytes accessed | tf_op | source)
XLA Modules:
  0.0 419.1 jit_solution(9212171889300298580)
XLA Ops:
  7.2 4.8 %copy.12 = bf16[2,256,3072]{1,2,0:T(8,128)(2,1)} copy(bf16[2,256,3072]{2,1,0:T(8,128)(2,1)} %param.5) | data formatting | bytes 6291456 | tf_op args[1]
  12.1 86.6 %all-gather.3.cloned.1.call-done = bf16[2,1024,3072]{1,2,0:T(8,128)(2,1)} async-done(((bf16[2,256,3072]{1,2,0:T(8,128)(2,1)}), bf16[2,1024,3072]{1,2,0:T(8,128)(2,1)}) %all-gather.3.cloned.1.call-update) | async-done | bytes 12582928 | tf_op jit(solution)/shard_map/all_gather | solution.py:27
  98.7 19.3 %convert_add_fusion = f32[2,3072,768]{2,1,0:T(8,128)} fusion(bf16[2,3072,768]{2,1,0:T(8,128)(2,1)} %param.6, bf16[2,1024,3072]{1,2,0:T(8,128)(2,1)} %all-gather.3.cloned.1.call-done, bf16[2,1024,768]{2,1,0:T(8,128)(2,1)S(1)} %copy-done), kind=kOutput, calls=%fused_computation.2 | convolution fusion | flops 9673113600 | bytes 44040192 | tf_op jit(solution)/shard_map/ltd,lte->lde/dot_general | solution.py:25
  118.0 22.5 %convolution_bitcast_fusion = f32[2,64,3072]{2,1,0:T(8,128)} fusion(f32[2,3072,768]{2,1,0:T(8,128)} %convert_add_fusion, f32[2,64,768]{2,1,0:T(8,128)S(1)} %copy-done.4), kind=kOutput, calls=%fused_computation.3 | convolution fusion | flops 3623878656 | bytes 20840448 | tf_op jit(solution)/shard_map/lre,lde->lrd/dot_general | solution.py:32
  140.5 28.1 %reduce-scatter.2.cloned.1.call-done = f32[2,64,768]{2,1,0:T(8,128)} async-done(((f32[2,64,3072]{2,1,0:T(8,128)}), f32[2,64,768]{2,1,0:T(8,128)}) %reduce-scatter.2.cloned.1.call-update) | async-done | bytes 393232 | tf_op jit(solution)/shard_map/reduce_scatter | solution.py:33
  168.7 0.1 copy.15
  168.9 75.0 %all-reduce.3.cloned.1.call-done = f32[2,64,768]{2,1,0:T(8,128)} async-done(((f32[2,64,768]{2,1,0:T(8,128)}), f32[2,64,768]{2,1,0:T(8,128)}) %all-reduce.3.cloned.1.call-update) | async-done | bytes 393232 | tf_op jit(solution)/shard_map/psum | solution.py:34
  243.9 1.7 fusion.10
  245.5 10.9 %psum.22 = f32[2,64,64]{1,2,0:T(8,128)S(1)} all-reduce(f32[2,64,64]{1,2,0:T(8,128)S(1)} %fusion.10), channel_id=1, replica_groups=mesh['dp'=8,'tensor'=4] {'tensor'}, use_global_device_ids=true, to_apply=%region_2.0 | all-reduce | flops 8192 | bytes 65536 | tf_op jit(solution)/shard_map/psum | solution.py:35
  256.4 1.9 copy.14
  258.3 0.9 gather_fusion
  259.3 0.1 multiply_add_fusion
  259.3 0.1 copy.16
  259.4 0.1 fusion.6
  259.5 11.7 %custom-call.8 = f32[2,64,64]{2,1,0:T(8,128)S(1)} custom-call(f32[2,64,64]{2,1,0:T(8,128)S(1)} %fusion.6), custom_call_target="Cholesky" | custom-call | tf_op jit(solution)/shard_map/jit(cholesky)/cholesky | solution.py:11
  271.3 0.1 compare_reduce_fusion
  271.4 0.1 select_bitcast_fusion
  271.5 9.8 %custom-call.9 = f32[2,1,64,64]{2,3,1,0:T(8,128)S(1)} custom-call(f32[2,1,64,64]{3,2,1,0:T(8,128)S(1)} %select_bitcast_fusion), custom_call_target="InvertDiagBlocksLowerTriangular" | custom-call | tf_op jit(solution)/shard_map/vmap(jit(_solve_triangular))/triangular_solve | solution.py:14
  281.3 1.3 fusion.4
  282.7 18.8 %all-gather.5.cloned.1.call-done = f32[2,64,3072]{2,1,0:T(8,128)} async-done(((f32[2,64,768]{2,1,0:T(8,128)}), f32[2,64,3072]{2,1,0:T(8,128)}) %all-gather.5.cloned.1.call-update) | async-done | bytes 1572880 | tf_op jit(solution)/shard_map/all_gather | solution.py:37
  301.5 16.3 %convolution_convert_fusion.1 = bf16[2,64,768]{2,1,0:T(8,128)(2,1)} fusion(f32[2,64,3072]{2,1,0:T(8,128)} %all-gather.5.cloned.1.call-done, f32[2,3072,768]{2,1,0:T(8,128)} %convert_add_fusion), kind=kOutput, calls=%fused_computation.5 | convolution fusion | flops 3623976960 | bytes 20643840 | tf_op jit(solution)/shard_map/lrd,lde->lre/dot_general | solution.py:38
  317.8 70.8 %all-reduce.5.cloned.1.call-done = bf16[2,64,768]{2,1,0:T(8,128)(2,1)} async-done(((bf16[2,64,768]{2,1,0:T(8,128)(2,1)}), bf16[2,64,768]{2,1,0:T(8,128)(2,1)}) %all-reduce.5.cloned.1.call-update) | async-done | bytes 196624 | tf_op jit(solution)/shard_map/psum | solution.py:39
  388.6 20.9 %subtract_convert_fusion = bf16[2,3072,768]{2,1,0:T(8,128)(2,1)} fusion(f32[2,3072,768]{2,1,0:T(8,128)} %convert_add_fusion, f32[2,64,3072]{2,1,0:T(8,128)} %all-gather.5.cloned.1.call-done, bf16[2,64,768]{2,1,0:T(8,128)(2,1)} %all-reduce.5.cloned.1.call-done), kind=kOutput, calls=%fused_computation.1 | convolution fusion | flops 3633512448 | bytes 30081024 | tf_op jit(solution)/shard_map/lrd,lre->lde/dot_general | solution.py:46
  409.5 3.1 convolution_convert_fusion
  (27 shorter events, 0.4 us)
Async XLA Ops:
  7.2 91.5 %copy-start = (bf16[2,1024,768]{2,1,0:T(8,128)(2,1)S(1)}, bf16[2,1024,768]{2,1,0:T(8,128)(2,1)}, u32[]{:S(2)}) copy-start(bf16[2,1024,768]{2,1,0:T(8,128)(2,1)} %param.4) | copy-start | bytes 9437188
  7.2 91.5 %all-gather.3.cloned.1.call-start = ((), (), s32[]{:S(2)}) async-start(), calls=%async_computation.1 | async-start | bytes 15728640 | tf_op jit(solution)/shard_map/all_gather | solution.py:27
  12.0 105.9 %copy-start.4 = (f32[2,64,768]{2,1,0:T(8,128)S(1)}, f32[2,64,768]{2,1,0:T(8,128)}, u32[]{:S(2)}) copy-start(f32[2,64,768]{2,1,0:T(8,128)} %param.7) | copy-start | bytes 1179652
  12.0 156.6 %reduce-scatter.2.cloned.1.call-start = ((), (), s32[]{:S(2)}) async-start(), calls=%async_computation.2 | async-start | bytes 1966080 | tf_op jit(solution)/shard_map/reduce_scatter | solution.py:33
  140.5 103.4 %all-reduce.3.cloned.1.call-start = ((), (), s32[]{:S(2)}) async-start(), calls=%async_computation.3 | async-start | bytes 786432 | tf_op jit(solution)/shard_map/psum | solution.py:34
  168.7 132.8 %all-gather.5.cloned.1.call-start = ((), (), s32[]{:S(2)}) async-start(), calls=%async_computation.4 | async-start | bytes 1966080 | tf_op jit(solution)/shard_map/all_gather | solution.py:37
  243.9 37.5 %copy-start.2 = (f32[2,64,768]{2,1,0:T(8,128)S(1)}, f32[2,64,768]{2,1,0:T(8,128)}, u32[]{:S(2)}) copy-start(f32[2,64,768]{2,1,0:T(8,128)} %all-reduce.3.cloned.1.call-done) | copy-start | bytes 1179652
  282.6 106.0 %all-reduce.5.cloned.1.call-start = ((), (), s32[]{:S(2)}) async-start(), calls=%async_computation.5 | async-start | bytes 393216 | tf_op jit(solution)/shard_map/psum | solution.py:39
  388.6 20.9 %copy-start.3 = (bf16[2,64,768]{2,1,0:T(8,128)(2,1)S(1)}, bf16[2,64,768]{2,1,0:T(8,128)(2,1)}, u32[]{:S(2)}) copy-start(bf16[2,64,768]{2,1,0:T(8,128)(2,1)} %all-reduce.5.cloned.1.call-done) | copy-start | bytes 589828
  388.6 24.0 %copy-start.1 = (bf16[2,1024,768]{2,1,0:T(8,128)(2,1)S(1)}, bf16[2,1024,768]{2,1,0:T(8,128)(2,1)}, u32[]{:S(2)}) copy-start(bf16[2,1024,768]{2,1,0:T(8,128)(2,1)} %param.4) | copy-start | bytes 9437188
Sparse Core Ops, SparseCore 0:
  12.2 86.4 all-gather.2
  140.6 27.9 reduce-scatter.1
  172.0 71.8 all-reduce.2
  282.8 18.6 all-gather.4
  317.9 70.6 all-reduce.4
where the time goes:
time: 419 us
  waiting for transfers between devices  279 us (67%)
  matrix products  85 us (20%)
  other arithmetic  22 us (5%)
  between operations  13.9 us (3%)
  blocking collectives  10.9 us (3%)
  local copies, waits for them, and re-layouts  7.81 us (2%)
    all_gather x1, waiting for transfers between devices, compress(): lax.all_gather(out_grad, 'tensor', axis=1, tiled=True)  86.6 us
    psum x1, waiting for transfers between devices, compress(): left_part = lax.psum(left_part, 'dp')  75 us
    psum x1, waiting for transfers between devices, compress(): lax.psum(right_terms.astype(jnp.bfloat16), 'dp').astype(jnp.float32)  70.8 us
    reduce_scatter x1, waiting for transfers between devices, compress(): lax.psum_scatter(left_factor, 'tensor', scatter_dimension=2, tiled=True)  28.1 us
    dot_general x1, matrix products, compress(): jnp.einsum('lre,lde->lrd', right_init, moment, precision=lax.Precision.HI...  22.5 us
    dot_general x1, matrix products, compress(): jnp.einsum('lrd,lre->lde', ortho_basis, right_factor / replicas, precisio...  20.9 us
    dot_general x1, matrix products, compress(): jnp.einsum('ltd,lte->lde', lax.all_gather(out_grad, 'tensor', axis=1, til...  19.3 us
    all_gather x1, waiting for transfers between devices, compress(): ortho_basis = lax.all_gather(ortho_part, 'tensor', axis=2, tiled=True)  18.8 us
  transfers between devices with their start and end apart: 5, of which 5 were waited for; matrix products, arithmetic and copies ran while one was open for 0% of the time, Pallas kernels for 0%

commit v1 on v0

--- a/solution.py
+++ b/solution.py
@@ -24,7 +24,7 @@
     out_width = out_grad.shape[2]
     moment = jnp.einsum(
         "ltd,lte->lde",
-        lax.all_gather(out_grad, "tensor", axis=1, tiled=True),
+        jnp.concatenate(lax.all_gather(out_grad, "tensor"), axis=1),
         context,
         preferred_element_type=jnp.float32,
     )

time: 419 us -> 458 us (1.093)
  local copies, waits for them, and re-layouts: 7.81 us -> 43.9 us
    reshape x0 -> x1, local copies, waits for them, and re-layouts: none -> 20.8 us  [compress(): jnp.concatenate(lax.all_gather(out_grad, 'tensor'), axis=1)]
    all_gather x0 -> x1, local copies, waits for them, and re-layouts: none -> 20.1 us  [compress(): lax.all_gather(out_grad, 'tensor')]
    unnamed x11 -> x8, local copies, waits for them, and re-layouts: 4.83 us -> 0.03 us
where the time goes in v1:
time: 458 us; the launch traced here: 457 us
  waiting for transfers between devices  280 us (61%)
  matrix products  85.9 us (19%)
  local copies, waits for them, and re-layouts  43.9 us (10%)
  other arithmetic  22 us (5%)
  between operations  13.9 us (3%)
  blocking collectives  10.9 us (2%)
    all_gather x1, waiting for transfers between devices, compress(): lax.all_gather(out_grad, 'tensor')  86.4 us
    psum x1, waiting for transfers between devices, compress(): left_part = lax.psum(left_part, 'dp')  74.9 us
    psum x1, waiting for transfers between devices, compress(): lax.psum(right_terms.astype(jnp.bfloat16), 'dp').astype(jnp.float32)  70.8 us
    reduce_scatter x1, waiting for transfers between devices, compress(): lax.psum_scatter(left_factor, 'tensor', scatter_dimension=2, tiled=True)  28.1 us
    dot_general x1, matrix products, compress(): jnp.einsum('lre,lde->lrd', right_init, moment, precision=lax.Precision.HI...  22.5 us
    reshape x1, local copies, waits for them, and re-layouts, compress(): jnp.concatenate(lax.all_gather(out_grad, 'tensor'), axis=1)  20.8 us
    dot_general x1, matrix products, compress(): jnp.einsum('lrd,lre->lde', ortho_basis, right_factor / replicas, precisio...  20.8 us
    all_gather x1, local copies, waits for them, and re-layouts, compress(): lax.all_gather(out_grad, 'tensor')  20.1 us
  transfers between devices with their start and end apart: 5, of which 5 were waited for; matrix products, arithmetic and copies ran while one was open for 0% of the time, Pallas kernels for 0%

profile of v1, /device:TPU:0, one launch (start us, length us, event | category | flops | bytes accessed | tf_op | source)
XLA Modules:
  0.0 456.6 jit_solution(11815629552688774967)
XLA Ops:
  7.2 0.7 all-gather.6.cloned.1.call-update
  8.0 86.4 %all-gather.6.cloned.1.call-done = bf16[8,256,3072]{2,1,0:T(8,128)(2,1)} async-done(((bf16[2,256,3072]{2,1,0:T(8,128)(2,1)}), bf16[8,256,3072]{2,1,0:T(8,128)(2,1)}) %all-gather.6.cloned.1.call-update) | async-done | bytes 12582928 | tf_op jit(solution)/shard_map/all_gather | solution.py:27
  94.4 20.1 %copy.18 = bf16[4,2,256,3072]{2,0,3,1:T(4,128)(2,1)} copy(bf16[4,2,256,3072]{3,2,1,0:T(8,128)(2,1)} %bitcast.29) | data formatting | bytes 25165824 | tf_op jit(solution)/shard_map/all_gather | solution.py:27
  114.5 20.8 %reshape.33 = bf16[2,1024,3072]{1,2,0:T(8,128)(2,1)} reshape(bf16[2,4,256,3072]{2,1,3,0:T(4,128)(2,1)} %bitcast.28) | data formatting | bytes 25165824 | tf_op jit(solution)/shard_map/reshape | solution.py:27
  135.3 19.3 %convert_add_fusion = f32[2,3072,768]{2,1,0:T(8,128)} fusion(bf16[2,3072,768]{2,1,0:T(8,128)(2,1)} %param.6, bf16[2,1024,3072]{1,2,0:T(8,128)(2,1)} %reshape.33, bf16[2,1024,768]{2,1,0:T(8,128)(2,1)S(1)} %copy-done), kind=kOutput, calls=%fused_computation.2 | convolution fusion | flops 9673113600 | bytes 44040192 | tf_op jit(solution)/shard_map/ltd,lte->lde/dot_general | solution.py:25
  154.6 22.5 %convolution_bitcast_fusion = f32[2,64,3072]{2,1,0:T(8,128)} fusion(f32[2,3072,768]{2,1,0:T(8,128)} %convert_add_fusion, f32[2,64,768]{2,1,0:T(8,128)S(1)} %copy-done.3), kind=kOutput, calls=%fused_computation.3 | convolution fusion | flops 3623878656 | bytes 20840448 | tf_op jit(solution)/shard_map/lre,lde->lrd/dot_general | solution.py:32
  177.2 28.1 %reduce-scatter.2.cloned.1.call-done = f32[2,64,768]{2,1,0:T(8,128)} async-done(((f32[2,64,3072]{2,1,0:T(8,128)}), f32[2,64,768]{2,1,0:T(8,128)}) %reduce-scatter.2.cloned.1.call-update) | async-done | bytes 393232 | tf_op jit(solution)/shard_map/reduce_scatter | solution.py:33
  205.5 74.9 %all-reduce.3.cloned.1.call-done = f32[2,64,768]{2,1,0:T(8,128)} async-done(((f32[2,64,768]{2,1,0:T(8,128)}), f32[2,64,768]{2,1,0:T(8,128)}) %all-reduce.3.cloned.1.call-update) | async-done | bytes 393232 | tf_op jit(solution)/shard_map/psum | solution.py:34
  280.4 1.6 fusion.10
  282.1 10.9 %psum.22 = f32[2,64,64]{1,2,0:T(8,128)S(1)} all-reduce(f32[2,64,64]{1,2,0:T(8,128)S(1)} %fusion.10), channel_id=1, replica_groups=mesh['dp'=8,'tensor'=4] {'tensor'}, use_global_device_ids=true, to_apply=%region_2.0 | all-reduce | flops 8192 | bytes 65536 | tf_op jit(solution)/shard_map/psum | solution.py:35
  292.9 1.9 copy.20
  294.9 0.9 gather_fusion
  295.9 0.1 copy.22
  296.0 0.1 fusion.6
  296.1 11.7 %custom-call.8 = f32[2,64,64]{2,1,0:T(8,128)S(1)} custom-call(f32[2,64,64]{2,1,0:T(8,128)S(1)} %fusion.6), custom_call_target="Cholesky" | custom-call | tf_op jit(solution)/shard_map/jit(cholesky)/cholesky | solution.py:11
  307.8 0.1 compare_reduce_fusion
  308.0 0.1 select_bitcast_fusion
  308.0 9.8 %custom-call.9 = f32[2,1,64,64]{2,3,1,0:T(8,128)S(1)} custom-call(f32[2,1,64,64]{3,2,1,0:T(8,128)S(1)} %select_bitcast_fusion), custom_call_target="InvertDiagBlocksLowerTriangular" | custom-call | tf_op jit(solution)/shard_map/vmap(jit(_solve_triangular))/triangular_solve | solution.py:14
  317.9 2.3 fusion.4
  320.2 18.8 %all-gather.4.cloned.1.call-done = f32[2,64,3072]{2,1,0:T(8,128)} async-done(((f32[2,64,768]{2,1,0:T(8,128)}), f32[2,64,3072]{2,1,0:T(8,128)}) %all-gather.4.cloned.1.call-update) | async-done | bytes 1572880 | tf_op jit(solution)/shard_map/all_gather | solution.py:37
  339.0 16.3 %convolution_convert_fusion.1 = bf16[2,64,768]{2,1,0:T(8,128)(2,1)} fusion(f32[2,64,3072]{2,1,0:T(8,128)} %all-gather.4.cloned.1.call-done, f32[2,3072,768]{2,1,0:T(8,128)} %convert_add_fusion), kind=kOutput, calls=%fused_computation.5 | convolution fusion | flops 3623976960 | bytes 20643840 | tf_op jit(solution)/shard_map/lrd,lde->lre/dot_general | solution.py:38
  355.4 70.8 %all-reduce.5.cloned.1.call-done = bf16[2,64,768]{2,1,0:T(8,128)(2,1)} async-done(((bf16[2,64,768]{2,1,0:T(8,128)(2,1)}), bf16[2,64,768]{2,1,0:T(8,128)(2,1)}) %all-reduce.5.cloned.1.call-update) | async-done | bytes 196624 | tf_op jit(solution)/shard_map/psum | solution.py:39
  426.2 20.8 %subtract_convert_fusion = bf16[2,3072,768]{2,1,0:T(8,128)(2,1)} fusion(f32[2,3072,768]{2,1,0:T(8,128)} %convert_add_fusion, f32[2,64,3072]{2,1,0:T(8,128)} %all-gather.4.cloned.1.call-done, bf16[2,64,768]{2,1,0:T(8,128)(2,1)} %all-reduce.5.cloned.1.call-done), kind=kOutput, calls=%fused_computation.1 | convolution fusion | flops 3633512448 | bytes 30081024 | tf_op jit(solution)/shard_map/lrd,lre->lde/dot_general | solution.py:46
  446.9 3.1 convolution_convert_fusion
  (26 shorter events, 0.5 us)
Async XLA Ops:
  7.2 128.1 %copy-start = (bf16[2,1024,768]{2,1,0:T(8,128)(2,1)S(1)}, bf16[2,1024,768]{2,1,0:T(8,128)(2,1)}, u32[]{:S(2)}) copy-start(bf16[2,1024,768]{2,1,0:T(8,128)(2,1)} %param.4) | copy-start | bytes 9437188
  7.2 87.2 %all-gather.6.cloned.1.call-start = ((), (), s32[]{:S(2)}) async-start(), calls=%async_computation.5 | async-start | bytes 15728640 | tf_op jit(solution)/shard_map/all_gather | solution.py:27
  7.9 197.4 %reduce-scatter.2.cloned.1.call-start = ((), (), s32[]{:S(2)}) async-start(), calls=%async_computation.1 | async-start | bytes 1966080 | tf_op jit(solution)/shard_map/reduce_scatter | solution.py:33
  135.3 19.3 %copy-start.3 = (f32[2,64,768]{2,1,0:T(8,128)S(1)}, f32[2,64,768]{2,1,0:T(8,128)}, u32[]{:S(2)}) copy-start(f32[2,64,768]{2,1,0:T(8,128)} %param.7) | copy-start | bytes 1179652
  177.1 103.3 %all-reduce.3.cloned.1.call-start = ((), (), s32[]{:S(2)}) async-start(), calls=%async_computation.2 | async-start | bytes 786432 | tf_op jit(solution)/shard_map/psum | solution.py:34
  205.3 133.7 %all-gather.4.cloned.1.call-start = ((), (), s32[]{:S(2)}) async-start(), calls=%async_computation.3 | async-start | bytes 1966080 | tf_op jit(solution)/shard_map/all_gather | solution.py:37
  320.2 106.0 %all-reduce.5.cloned.1.call-start = ((), (), s32[]{:S(2)}) async-start(), calls=%async_computation.4 | async-start | bytes 393216 | tf_op jit(solution)/shard_map/psum | solution.py:39
  355.3 94.7 %copy-start.1 = (bf16[2,1024,768]{2,1,0:T(8,128)(2,1)S(1)}, bf16[2,1024,768]{2,1,0:T(8,128)(2,1)}, u32[]{:S(2)}) copy-start(bf16[2,1024,768]{2,1,0:T(8,128)(2,1)} %param.4) | copy-start | bytes 9437188
  426.2 20.8 %copy-start.2 = (bf16[2,64,768]{2,1,0:T(8,128)(2,1)S(1)}, bf16[2,64,768]{2,1,0:T(8,128)(2,1)}, u32[]{:S(2)}) copy-start(bf16[2,64,768]{2,1,0:T(8,128)(2,1)} %all-reduce.5.cloned.1.call-done) | copy-start | bytes 589828
Sparse Core Ops, SparseCore 0:
  9.5 84.7 all-gather.5
  177.3 27.9 reduce-scatter.1
  208.6 71.7 all-reduce.2
  320.3 18.6 all-gather.3
  355.5 70.6 all-reduce.4
